TPU v7x, 32 devices: a whole 2x2x4 slice. The times are simulated.
32 devices in a mesh: group: 2 (over y), seq: 4 (over z), fsdp: 4 (over x, core).
Axes of the slice: x: 2, y: 2, z: 4, core: 2. Of those that a mesh axis runs over, the one named last changes fastest.
Arguments:
- tile_patches: bfloat16 [64, 256, 1536], P(('group', 'seq', 'fsdp')), parts along dimension 0, may hold values from -6 to 6
- vit_gain: float32 [1536], replicated, may hold values from 0.25 to 1.75
- w_query: bfloat16 [1536, 768], P('fsdp'), may hold values from -0.15625 to 0.15625
- w_key: bfloat16 [1536, 768], P('fsdp'), may hold values from -0.15625 to 0.15625
- w_value: bfloat16 [1536, 768], P('fsdp'), may hold values from -0.15625 to 0.15625
- w_out: bfloat16 [768, 1536], P('fsdp'), may hold values from -0.21875 to 0.21875
- w_proj: bfloat16 [1536, 768], P('fsdp'), may hold values from -0.15625 to 0.15625
- long_gain: float32 [768], replicated, may hold values from 0.25 to 1.75
- long_query: bfloat16 [768, 768], P(None, 'fsdp'), may hold values from -0.21875 to 0.21875
- long_key: bfloat16 [768, 768], P(None, 'fsdp'), may hold values from -0.21875 to 0.21875
- long_value: bfloat16 [768, 768], P(None, 'fsdp'), may hold values from -0.21875 to 0.21875
- long_out: bfloat16 [768, 768], P('fsdp'), may hold values from -0.21875 to 0.21875
- seq_order: int32 [64], P(('group', 'seq', 'fsdp')), parts along dimension 0, may hold values from 0 to 31, each once
- counts: int32 [32], P(('group', 'seq', 'fsdp')), parts along dimension 0, may hold values from 1 to 2
Outputs:
- encoded: bfloat16 [64, 768], P(('group', 'seq'), 'fsdp'), parts along dimension 0
There are 2 independent parts, one for each index of `group`. A program takes and returns all parts, laid end to end along the dimension named above; an argument that names none is the same for every part. Nothing has to cross between parts.
Inputs may be any that keep to these rules, and one draw needn't show every extreme that they name: `seq_order`: each of the 32 sequence positions belongs to exactly one tile. In each block of 2 consecutive tiles the first counts tiles are tissue.
All inputs are finite; a program needn't handle non-finite values.
Results may differ from a plain program's by a relative error of at most 0.013.
Values may be sent and summed in bfloat16 or wider, within the bound.
No kernel may reach another device: no remote copies, remote signals or barrier semaphores. Data moves between devices by JAX's collectives and lax.ppermute only.
A program may use at most 64 MiB of HBM per device.

v0:
```python
import math
import jax
import jax.numpy as jnp
from jax import lax
from jax.sharding import PartitionSpec as P

VHD = 64
HEADS = 16
DILATION_STEP = 4
EPSILON = 1e-06


def layer_norm(inputs, norm_gain):
    widened = inputs.astype(jnp.float32)
    average = jnp.mean(widened, axis=-1, keepdims=True)
    centred = widened - average
    variance = jnp.mean(centred * centred, axis=-1, keepdims=True)
    return (centred * lax.rsqrt(variance + EPSILON) * norm_gain).astype(jnp.bfloat16)


def dilated_attention(
    query_rows,
    key_rows,
    value_rows,
    query_position_index,
    key_position_index,
    key_present,
    leading_head,
    head_total_count,
    segment,
):
    head_size = query_rows.shape[1] // head_total_count
    query_heads = query_rows.reshape(query_rows.shape[0], head_total_count, head_size)
    key_heads = key_rows.reshape(key_rows.shape[0], head_total_count, head_size)
    value_heads = value_rows.reshape(value_rows.shape[0], head_total_count, head_size)
    scores = jnp.einsum(
        "rhd,khd->hrk", query_heads, key_heads, preferred_element_type=jnp.float32
    ) / math.sqrt(head_size)
    itself = query_position_index[:, None] == key_position_index[None, :]
    permitted_mask = (key_present[None, :] > 0) | itself
    in_local = (
        query_position_index[:, None] // segment == key_position_index[None, :] // segment
    ) & permitted_mask
    head_shift_amounts = (
        leading_head + jnp.arange(head_total_count, dtype=jnp.int32)
    ) % DILATION_STEP
    within_dilated_set = (
        ((query_position_index % DILATION_STEP)[None, :, None] == head_shift_amounts[:, None, None])
        & ((key_position_index % DILATION_STEP)[None, None, :] == head_shift_amounts[:, None, None])
        & permitted_mask[None]
    )
    lifted = jnp.exp(scores)
    local_weights = jnp.where(in_local[None], lifted, 0.0)
    dilated_weights = jnp.where(within_dilated_set, lifted, 0.0)
    denominator = jnp.sum(local_weights, axis=-1) + jnp.sum(dilated_weights, axis=-1)
    numerator = jnp.einsum(
        "hrk,khd->rhd",
        local_weights.astype(jnp.bfloat16),
        value_heads,
        preferred_element_type=jnp.float32,
    )
    numerator = numerator + jnp.einsum(
        "hrk,khd->rhd",
        dilated_weights.astype(jnp.bfloat16),
        value_heads,
        preferred_element_type=jnp.float32,
    )
    combined = numerator / jnp.transpose(denominator)[:, :, None]
    return combined.reshape(query_rows.shape[0], head_total_count * head_size).astype(jnp.bfloat16)


def local(
    tile_patches,
    vit_gain,
    w_query,
    w_key,
    w_value,
    w_out,
    w_proj,
    long_gain,
    long_query,
    long_key,
    long_value,
    long_out,
    seq_order,
    counts,
):
    seq_size = lax.axis_size("seq")
    group_size = lax.axis_size("fsdp")
    tile_count, patch_count, width = tile_patches.shape
    normed = layer_norm(tile_patches, vit_gain)
    class_normed = normed[:, 0, :]
    vit_width = w_key.shape[1]
    vit_heads = vit_width // VHD
    full_query, full_out, full_proj = (
        lax.all_gather(w_query, "fsdp", axis=0, tiled=True),
        lax.all_gather(w_out, "fsdp", axis=0, tiled=True),
        lax.all_gather(w_proj, "fsdp", axis=0, tiled=True),
    )
    query_row = jnp.dot(class_normed, full_query, preferred_element_type=jnp.float32).astype(
        jnp.bfloat16
    )
    group_query = lax.all_gather(query_row, "fsdp", axis=0, tiled=True)
    rows_local = w_key.shape[0]
    key_heads_local = w_key.reshape(rows_local, vit_heads, VHD)
    query_group = group_query.reshape(group_query.shape[0], vit_heads, VHD)
    key_part = jnp.einsum(
        "ihd,thd->thi", key_heads_local, query_group, preferred_element_type=jnp.float32
    )
    folded = lax.all_to_all(
        key_part.astype(jnp.bfloat16), "fsdp", split_axis=0, concat_axis=2, tiled=True
    ).astype(key_part.dtype)
    scores = jnp.einsum(
        "tpi,thi->thp", normed.astype(jnp.float32), folded, precision=lax.Precision.HIGHEST
    ) / math.sqrt(VHD)
    lifted = jnp.exp(scores)
    attn_probs = (lifted / jnp.sum(lifted, axis=-1, keepdims=True)).astype(jnp.bfloat16)
    mixed = jnp.einsum("thp,tpi->thi", attn_probs, normed, preferred_element_type=jnp.float32)
    spread_rows = lax.all_to_all(
        mixed.astype(jnp.bfloat16), "fsdp", split_axis=2, concat_axis=0, tiled=True
    ).astype(mixed.dtype)
    value_heads_local = w_value.reshape(rows_local, vit_heads, VHD).astype(jnp.float32)
    summed_heads = jnp.einsum(
        "thi,ihd->thd", spread_rows, value_heads_local, precision=lax.Precision.HIGHEST
    )
    pooled = lax.psum_scatter(
        summed_heads.reshape(tile_count * lax.axis_size("fsdp"), vit_width).astype(jnp.bfloat16),
        "fsdp",
        scatter_dimension=0,
        tiled=True,
    ).astype(jnp.float32)
    pooled = pooled.astype(jnp.bfloat16)
    class_input = tile_patches[:, 0, :].astype(jnp.float32)
    class_row = (
        class_input + jnp.dot(pooled, full_out, preferred_element_type=jnp.float32)
    ).astype(jnp.bfloat16)
    embeds = jnp.dot(class_row, full_proj, preferred_element_type=jnp.float32).astype(jnp.bfloat16)
    tile_slot = jnp.arange(tile_count, dtype=jnp.int32)
    present = (tile_slot < counts[0]).astype(jnp.int32)
    embeds = jnp.where(present[:, None] > 0, embeds, jnp.zeros_like(embeds))
    model_width = embeds.shape[1]
    rows_dev = tile_count * group_size
    total_tiles = rows_dev * seq_size
    segment = total_tiles // 4
    head_width = long_query.shape[1]
    heads_dev = head_width // (model_width // HEADS)
    leading_head = lax.axis_index("fsdp") * heads_dev
    targets = lax.axis_index("seq") * rows_dev + jnp.arange(rows_dev, dtype=jnp.int32)
    column_start = lax.axis_index("fsdp") * head_width
    all_embeds, all_order, all_present = (
        lax.all_gather(embeds, ("seq", "fsdp"), axis=0, tiled=True),
        lax.all_gather(seq_order, ("seq", "fsdp"), axis=0, tiled=True),
        lax.all_gather(present, ("seq", "fsdp"), axis=0, tiled=True),
    )
    picker = all_order[None, :] == targets[:, None]
    mine = jnp.dot(
        picker.astype(jnp.bfloat16), all_embeds, preferred_element_type=jnp.float32
    ).astype(jnp.bfloat16)
    mine_present = jnp.sum(jnp.where(picker, all_present[None, :], 0), axis=1).astype(jnp.int32)
    long_normed = layer_norm(mine, long_gain)
    query_rows = jnp.dot(long_normed, long_query, preferred_element_type=jnp.float32).astype(
        jnp.bfloat16
    )
    key_local = jnp.dot(long_normed, long_key, preferred_element_type=jnp.float32).astype(
        jnp.bfloat16
    )
    value_local = jnp.dot(long_normed, long_value, preferred_element_type=jnp.float32).astype(
        jnp.bfloat16
    )
    key_rows, value_rows, key_present = (
        lax.all_gather(key_local, "seq", axis=0, tiled=True),
        lax.all_gather(value_local, "seq", axis=0, tiled=True),
        lax.all_gather(mine_present, "seq", axis=0, tiled=True),
    )
    key_position_index = jnp.arange(total_tiles, dtype=jnp.int32)
    residual = lax.dynamic_slice_in_dim(mine, column_start, head_width, 1)
    attended = dilated_attention(
        query_rows,
        key_rows,
        value_rows,
        targets,
        key_position_index,
        key_present,
        leading_head,
        heads_dev,
        segment,
    )
    head_terms = jnp.dot(attended, long_out, preferred_element_type=jnp.float32)
    summed = lax.psum_scatter(
        head_terms.astype(jnp.bfloat16), "fsdp", scatter_dimension=1, tiled=True
    ).astype(jnp.float32)
    return (residual.astype(jnp.float32) + summed).astype(jnp.bfloat16)


def solution(mesh):
    return jax.shard_map(
        local,
        mesh=mesh,
        in_specs=(
            P(("group", "seq", "fsdp"), None, None),
            P(),
            P("fsdp", None),
            P("fsdp", None),
            P("fsdp", None),
            P("fsdp", None),
            P("fsdp", None),
            P(),
            P(None, "fsdp"),
            P(None, "fsdp"),
            P(None, "fsdp"),
            P("fsdp", None),
            P(("group", "seq", "fsdp")),
            P(("group", "seq", "fsdp")),
        ),
        out_specs=P(("group", "seq"), "fsdp"),
        check_vma=False,
    )
```

profile of v0, /device:TPU:0, one launch (start us, length us, event | category | flops | bytes accessed | tf_op | source)
XLA Modules:
  0.0 166.9 jit_solution(15862712524347487263)
XLA Ops:
  6.5 0.7 all-gather.6.cloned.1.call-update
  7.3 0.7 all-gather.10.cloned.1.call-update
  8.1 0.7 all-gather.8.cloned.1.call-update
  9.1 0.5 fusion.2
  10.3 0.5 fusion.4
  10.9 0.6 dynamic-slice
  12.3 2.1 %copy.37 = bf16[384,768]{0,1:T(8,128)(2,1)} copy(bf16[384,768]{1,0:T(8,128)(2,1)} %param.17) | data formatting | bytes 1179648 | tf_op args[3]
  14.4 0.6 dynamic-slice.2
  15.8 13.8 %all-reduce.4 = (s32[32]{0:T(128)S(1)}, s32[32]{0:T(128)S(1)}) all-reduce(s32[32]{0:T(128)S(1)} %dynamic-update-slice, s32[32]{0:T(128)S(1)} %fusion.55), channel_id=1, replica_groups=mesh['group'=2,'seq'=4,'fsdp'=4] {'seq','fsdp'}, use_global_device_ids=true, to_apply=%add | all-reduce | flops 64 | bytes 512
  30.0 6.2 %all-reduce.2 = s32[32]{0:T(128)S(1)} all-reduce(s32[32]{0:T(128)S(1)} %dynamic-update-slice.2), channel_id=1, replica_groups=mesh['group'=2,'seq'=4,'fsdp'=4] {'seq'}, use_global_device_ids=true, to_apply=%add.2 | all-reduce | flops 32 | bytes 256
  36.5 2.1 %fusion.17 = bf16[1,2,768]{2,1,0:T(2,128)(2,1)S(1)} fusion(bf16[1536,768]{1,0:T(8,128)(2,1)} %all-gather.6.cloned.1.call-done, bf16[2,1,1536]{2,1,0:T(2,128)(2,1)S(1)} %slice.8), kind=kOutput, calls=%fused_computation.32 | convolution fusion | flops 4720128 | bytes 2368512 | tf_op jit(solution)/shard_map/dot_general | solution.py:100
  38.6 5.2 %all-gather = bf16[4,2,768]{2,1,0:T(2,128)(2,1)S(1)} all-gather(bf16[1,2,768]{2,1,0:T(2,128)(2,1)S(1)} %fusion.17), channel_id=1, replica_groups=mesh['group'=2,'seq'=4,'fsdp'=4] {'fsdp'}, dimensions={0}, use_global_device_ids=true | all-gather | bytes 15360 | tf_op jit(solution)/shard_map/all_gather | solution.py:103
  44.1 0.7 copy.39
  44.8 3.3 %all-to-all-start = ((bf16[8,12,384]{2,1,0:T(8,128)(2,1)}), bf16[8,12,384]{2,1,0:T(8,128)(2,1)S(1)}, u32[]{:S(2)}, u32[]{:S(2)}) async-start(bf16[8,12,384]{2,1,0:T(8,128)(2,1)} %copy.39), calls=%async_computation | async-start | bytes 196608 | tf_op jit(solution)/shard_map/all_to_all | solution.py:110
  48.2 5.6 %all-to-all-done = bf16[8,12,384]{2,1,0:T(8,128)(2,1)S(1)} async-done(((bf16[8,12,384]{2,1,0:T(8,128)(2,1)}), bf16[8,12,384]{2,1,0:T(8,128)(2,1)S(1)}, u32[]{:S(2)}, u32[]{:S(2)}) %all-to-all-start) | async-done | bytes 73760 | tf_op jit(solution)/shard_map/all_to_all | solution.py:110
  54.8 0.6 copy.42
  55.4 2.1 %reshape.362 = bf16[4,2,4608]{2,1,0:T(2,128)(2,1)} reshape(bf16[1536,2,12]{2,1,0:T(2,128)(2,1)S(1)} %bitcast.61) | data formatting | bytes 147456
  57.5 3.3 %all-to-all-start.1 = ((bf16[4,2,4608]{2,1,0:T(2,128)(2,1)}), bf16[4,2,4608]{2,1,0:T(2,128)(2,1)S(1)}, u32[]{:S(2)}, u32[]{:S(2)}) async-start(bf16[4,2,4608]{2,1,0:T(2,128)(2,1)} %reshape.362), calls=%async_computation.1 | async-start | bytes 147456 | tf_op jit(solution)/shard_map/all_to_all | solution.py:119
  61.2 0.6 dynamic-slice.3
  62.5 2.5 %all-to-all-done.1 = bf16[4,2,4608]{2,1,0:T(2,128)(2,1)S(1)} async-done(((bf16[4,2,4608]{2,1,0:T(2,128)(2,1)}), bf16[4,2,4608]{2,1,0:T(2,128)(2,1)S(1)}, u32[]{:S(2)}, u32[]{:S(2)}) %all-to-all-start.1) | async-done | bytes 73760 | tf_op jit(solution)/shard_map/all_to_all | solution.py:119
  65.0 1.8 %reshape.363 = bf16[1536,2,12]{2,1,0:T(2,128)(2,1)S(1)} reshape(bf16[4,2,4608]{2,1,0:T(2,128)(2,1)S(1)} %all-to-all-done.1) | data formatting | bytes 147456
  66.8 0.6 copy.52
  67.9 10.9 %all-reduce.3 = bf16[8,768]{1,0:T(8,128)(2,1)S(1)} all-reduce(bf16[8,768]{1,0:T(8,128)(2,1)S(1)} %convert_element_type.110), channel_id=2, replica_groups=mesh['group'=2,'seq'=4,'fsdp'=4] {'fsdp'}, use_global_device_ids=true, to_apply=%region_3.0.clone | all-reduce | flops 6144 | bytes 24576
  78.9 9.4 %all-gather.8.cloned.1.call-done = bf16[768,1536]{1,0:T(8,128)(2,1)} async-done(((bf16[192,1536]{1,0:T(8,128)(2,1)}), bf16[768,1536]{1,0:T(8,128)(2,1)}) %all-gather.8.cloned.1.call-update) | async-done | bytes 2359312 | tf_op jit(solution)/shard_map/all_gather | solution.py:97
  88.3 3.2 %fusion.16 = bf16[1,2,768]{2,1,0:T(2,128)(2,1)S(1)} fusion(bf16[1536,768]{1,0:T(8,128)(2,1)} %all-gather.10.cloned.1.call-done, bf16[768,1536]{1,0:T(8,128)(2,1)} %all-gather.8.cloned.1.call-done, f32[2,1,1536]{2,1,0:T(1,128)S(1)} %slice_convert_fusion, pred[2]{0:T(512)(128)(4,1)S(1)} %fusion.56, bf16[8,768]{1,0:T(8,128)(2,1)S(1)} %all-reduce.3, ...), kind=kOutput, calls=%fused_computation.31 | convolution fusion | flops 9446400 | bytes 4737540 | tf_op jit(solution)/shard_map/dot_general | solution.py:137
  91.5 20.5 %all-gather.1 = bf16[16,2,768]{2,1,0:T(2,128)(2,1)S(1)} all-gather(bf16[1,2,768]{2,1,0:T(2,128)(2,1)S(1)} %fusion.16), channel_id=1, replica_groups=mesh['group'=2,'seq'=4,'fsdp'=4] {'seq','fsdp'}, dimensions={0}, use_global_device_ids=true | all-gather | bytes 52224 | tf_op jit(solution)/shard_map/all_gather | solution.py:151
  113.1 13.3 %all_gather.39 = bf16[32,192]{1,0:T(8,128)(2,1)S(1)} all-gather(bf16[8,192]{1,0:T(8,128)(2,1)S(1)} %convolution_convert_fusion.5), channel_id=1, replica_groups=mesh['group'=2,'seq'=4,'fsdp'=4] {'seq'}, dimensions={0}, use_global_device_ids=true | all-gather | bytes 15360 | tf_op jit(solution)/shard_map/all_gather | solution.py:171
  126.6 13.3 %all_gather.36 = bf16[32,192]{1,0:T(8,128)(2,1)S(1)} all-gather(bf16[8,192]{1,0:T(8,128)(2,1)S(1)} %convolution_convert_fusion.7), channel_id=1, replica_groups=mesh['group'=2,'seq'=4,'fsdp'=4] {'seq'}, dimensions={0}, use_global_device_ids=true | all-gather | bytes 15360 | tf_op jit(solution)/shard_map/all_gather | solution.py:172
  140.8 0.8 copy.53
  141.7 17.2 %reduce-scatter.4.cloned.1.call-done = bf16[192,8]{1,0:T(8,128)(2,1)} async-done(((bf16[768,8]{1,0:T(8,128)(2,1)}), bf16[192,8]{1,0:T(8,128)(2,1)}) %reduce-scatter.4.cloned.1.call-update) | async-done | bytes 3088
  158.8 0.8 copy.54
  159.7 0.7 add_convert_fusion
  (86 shorter events, 5.7 us)
Async XLA Ops:
  6.5 134.1 %copy-start = (bf16[192,768]{1,0:T(8,128)(2,1)S(1)}, bf16[192,768]{1,0:T(8,128)(2,1)}, u32[]{:S(2)}) copy-start(bf16[192,768]{1,0:T(8,128)(2,1)} %param.25) | copy-start | bytes 884740
  6.5 2.2 %copy-start.1 = (bf16[2,256,1536]{2,1,0:T(8,128)(2,1)S(1)}, bf16[2,256,1536]{2,1,0:T(8,128)(2,1)}, u32[]{:S(2)}) copy-start(bf16[2,256,1536]{2,1,0:T(8,128)(2,1)} %param.14) | copy-start | bytes 4718596
  6.5 3.8 %copy-start.4 = (f32[1536]{0:T(1024)S(1)}, f32[1536]{0:T(1024)}, u32[]{:S(2)}) copy-start(f32[1536]{0:T(1024)} %param.15) | copy-start | bytes 18436
  6.5 29.9 %all-gather.6.cloned.1.call-start = ((), (), s32[]{:S(2)}) async-start(), calls=%async_computation.3 | async-start | bytes 2949120 | tf_op jit(solution)/shard_map/all_gather | solution.py:96
  7.3 71.7 %all-gather.10.cloned.1.call-start = ((), (), s32[]{:S(2)}) async-start(), calls=%async_computation.5 | async-start | bytes 2949120 | tf_op jit(solution)/shard_map/all_gather | solution.py:98
  8.0 80.3 %all-gather.8.cloned.1.call-start = ((), (), s32[]{:S(2)}) async-start(), calls=%async_computation.4 | async-start | bytes 2949120 | tf_op jit(solution)/shard_map/all_gather | solution.py:97
  9.1 1.8 %copy-start.12 = (u32[32]{0:T(128)S(1)}, u32[32]{0:T(128)}, u32[]{:S(2)}) copy-start(u32[32]{0:T(128)} %constant.98) | copy-start | bytes 388
  9.6 4.8 %copy-start.11 = (u32[32]{0:T(128)S(1)}, u32[32]{0:T(128)}, u32[]{:S(2)}) copy-start(u32[32]{0:T(128)} %constant.108) | copy-start | bytes 388
  9.6 5.4 %copy-start.9 = (s32[2]{0:T(128)S(1)}, s32[2]{0:T(128)}, u32[]{:S(2)}) copy-start(s32[2]{0:T(128)} %param.26) | copy-start | bytes 28
  36.4 7.4 %copy-start.2 = (bf16[384,768]{0,1:T(8,128)(2,1)S(1)}, bf16[384,768]{0,1:T(8,128)(2,1)}, u32[]{:S(2)}) copy-start(bf16[384,768]{0,1:T(8,128)(2,1)} %copy.37) | copy-start | bytes 1769476
  44.8 9.0 %all-to-all-start = ((bf16[8,12,384]{2,1,0:T(8,128)(2,1)}), bf16[8,12,384]{2,1,0:T(8,128)(2,1)S(1)}, u32[]{:S(2)}, u32[]{:S(2)}) async-start(bf16[8,12,384]{2,1,0:T(8,128)(2,1)} %copy.39), calls=%async_computation | async-start | bytes 196608 | tf_op jit(solution)/shard_map/all_to_all | solution.py:110
  53.9 7.1 %copy-start.3 = (bf16[384,768]{1,0:T(8,128)(2,1)S(1)}, bf16[384,768]{1,0:T(8,128)(2,1)}, u32[]{:S(2)}) copy-start(bf16[384,768]{1,0:T(8,128)(2,1)} %param.18) | copy-start | bytes 1769476
  54.4 6.8 %copy-start.10 = (u32[32]{0:T(128)S(1)}, u32[32]{0:T(128)}, u32[]{:S(2)}) copy-start(u32[32]{0:T(128)} %constant.116) | copy-start | bytes 388
  57.5 7.4 %all-to-all-start.1 = ((bf16[4,2,4608]{2,1,0:T(2,128)(2,1)}), bf16[4,2,4608]{2,1,0:T(2,128)(2,1)S(1)}, u32[]{:S(2)}, u32[]{:S(2)}) async-start(bf16[4,2,4608]{2,1,0:T(2,128)(2,1)} %reshape.362), calls=%async_computation.1 | async-start | bytes 147456 | tf_op jit(solution)/shard_map/all_to_all | solution.py:119
  60.8 98.0 %reduce-scatter.4.cloned.1.call-start = ((), (), s32[]{:S(2)}) async-start(), calls=%async_computation.6 | async-start | bytes 245760
  78.9 33.7 %copy-start.5 = (bf16[768,192]{0,1:T(8,128)(2,1)S(1)}, bf16[768,192]{0,1:T(8,128)(2,1)}, u32[]{:S(2)}) copy-start(bf16[768,192]{0,1:T(8,128)(2,1)} %param.22) | copy-start | bytes 884740
  78.9 33.7 %copy-start.8 = (f32[768]{0:T(1024)S(1)}, f32[768]{0:T(1024)}, u32[]{:S(2)}) copy-start(f32[768]{0:T(1024)} %param.21) | copy-start | bytes 9220
  78.9 34.0 %copy-start.6 = (bf16[768,192]{0,1:T(8,128)(2,1)S(1)}, bf16[768,192]{0,1:T(8,128)(2,1)}, u32[]{:S(2)}) copy-start(bf16[768,192]{0,1:T(8,128)(2,1)} %param.23) | copy-start | bytes 884740
  78.9 47.6 %copy-start.7 = (bf16[768,192]{0,1:T(8,128)(2,1)S(1)}, bf16[768,192]{0,1:T(8,128)(2,1)}, u32[]{:S(2)}) copy-start(bf16[768,192]{0,1:T(8,128)(2,1)} %param.24) | copy-start | bytes 884740
Sparse Core Ops, SparseCore 0:
  8.9 26.8 all-gather.5
  37.3 25.1 all-gather.9
  64.1 24.1 all-gather.7
  141.8 16.9 reduce-scatter.3
where the time goes:
time: 167 us
  blocking collectives  83.2 us (50%)
  waiting for transfers between devices  36.8 us (22%)
  between operations  16.1 us (10%)
  local copies, waits for them, and re-layouts  13 us (8%)
  matrix products  8.27 us (5%)
  starting transfers between devices  6.71 us (4%)
  other arithmetic  2.85 us (2%)
    unnamed x3, blocking collectives  30.9 us
    all_gather x1, blocking collectives, local(): lax.all_gather(embeds, ('seq', 'fsdp'), axis=0, tiled=True)  20.5 us
    unnamed x5, waiting for transfers between devices  19.3 us
    all_gather x1, blocking collectives, local(): lax.all_gather(key_local, 'seq', axis=0, tiled=True)  13.3 us
    all_gather x1, blocking collectives, local(): lax.all_gather(value_local, 'seq', axis=0, tiled=True)  13.3 us
    unnamed x41, local copies, waits for them, and re-layouts  10.4 us
    all_gather x1, waiting for transfers between devices, local(): lax.all_gather(w_out, 'fsdp', axis=0, tiled=True)  9.38 us
    all_to_all x1, waiting for transfers between devices, local(): lax.all_to_all(key_part.astype(jnp.bfloat16), 'fsdp', split_axis=0, conca...  5.61 us
  transfers between devices with their start and end apart: 6, of which 4 were waited for; matrix products, arithmetic and copies ran while one was open for 10% of the time, Pallas kernels for 0%

commit v1 on v0

--- a/solution.py
+++ b/solution.py
@@ -8,6 +8,17 @@
 HEADS = 16
 DILATION_STEP = 4
 EPSILON = 1e-06
+
+
+def ring_gather(x, axis, dim):
+    ways = lax.axis_size(axis)
+    pieces = [x]
+    for far in range(1, ways):
+        pieces.append(
+            lax.ppermute(pieces[far - 1], axis, [(d, (d - 1) % ways) for d in range(ways)])
+        )
+    line = jnp.concatenate(pieces, axis=dim)
+    return jnp.roll(line, lax.axis_index(axis) * x.shape[dim], axis=dim)
 
 
 def layer_norm(inputs, norm_gain):
@@ -148,7 +159,7 @@
     targets = lax.axis_index("seq") * rows_dev + jnp.arange(rows_dev, dtype=jnp.int32)
     column_start = lax.axis_index("fsdp") * head_width
     all_embeds, all_order, all_present = (
-        lax.all_gather(embeds, ("seq", "fsdp"), axis=0, tiled=True),
+        ring_gather(embeds, ("seq", "fsdp"), 0),
         lax.all_gather(seq_order, ("seq", "fsdp"), axis=0, tiled=True),
         lax.all_gather(present, ("seq", "fsdp"), axis=0, tiled=True),
     )

time: 167 us -> 239 us (1.43)
  starting transfers between devices: 6.71 us -> 64.9 us
  waiting for transfers between devices: 36.8 us -> 74.8 us
  blocking collectives: 83.2 us -> 57.2 us
    ppermute x0 -> x15, starting transfers between devices: none -> 58.2 us  [ring_gather(): lax.ppermute(pieces[far - 1], axis, [(d, (d - 1) % ways) for d in range(w...]
    all_gather x1, waiting for transfers between devices: 0.02 us -> 23.4 us  [local(): lax.all_gather(w_query, 'fsdp', axis=0, tiled=True)]
    all_gather x1 -> x0, blocking collectives: 20.5 us -> none  [local(): lax.all_gather(embeds, ('seq', 'fsdp'), axis=0, tiled=True)]
    ppermute x0 -> x15, waiting for transfers between devices: none -> 15.6 us  [ring_gather(): lax.ppermute(pieces[far - 1], axis, [(d, (d - 1) % ways) for d in range(w...]
    all_gather x1, waiting for transfers between devices: 9.38 us -> 0.02 us  [local(): lax.all_gather(w_out, 'fsdp', axis=0, tiled=True)]
    all_gather x1, waiting for transfers between devices: 0.02 us -> 9.01 us  [local(): lax.all_gather(w_proj, 'fsdp', axis=0, tiled=True)]
    unnamed x3, blocking collectives: 30.9 us -> 25.4 us
    unnamed x41 -> x38, local copies, waits for them, and re-layouts: 10.4 us -> 10.5 us
  transfers between devices with their start and end apart: 6 -> 21, of which waited for: 4 -> 17; matrix products, arithmetic and copies ran while one was open for 10% -> 7% of each run, Pallas kernels for 0% -> 0%
where the time goes in v1:
time: 239 us; the launch traced here: 238 us
  waiting for transfers between devices  74.8 us (31%)
  starting transfers between devices  64.9 us (27%)
  blocking collectives  57.2 us (24%)
  between operations  16 us (7%)
  local copies, waits for them, and re-layouts  13.4 us (6%)
  matrix products  9.3 us (4%)
  other arithmetic  2.84 us (1%)
    ppermute x15, starting transfers between devices, ring_gather(): lax.ppermute(pieces[far - 1], axis, [(d, (d - 1) % ways) for d in range(w...  58.2 us
    unnamed x3, blocking collectives  25.4 us
    all_gather x1, waiting for transfers between devices, local(): lax.all_gather(w_query, 'fsdp', axis=0, tiled=True)  23.4 us
    unnamed x5, waiting for transfers between devices  19.3 us
    ppermute x15, waiting for transfers between devices, ring_gather(): lax.ppermute(pieces[far - 1], axis, [(d, (d - 1) % ways) for d in range(w...  15.6 us
    all_gather x1, blocking collectives, local(): lax.all_gather(key_local, 'seq', axis=0, tiled=True)  13.3 us
    all_gather x1, blocking collectives, local(): lax.all_gather(value_local, 'seq', axis=0, tiled=True)  13.3 us
    unnamed x38, local copies, waits for them, and re-layouts  10.5 us
  transfers between devices with their start and end apart: 21, of which 17 were waited for; matrix products, arithmetic and copies ran while one was open for 7% of the time, Pallas kernels for 0%

profile of v1, /device:TPU:0, one launch (start us, length us, event | category | flops | bytes accessed | tf_op | source)
XLA Modules:
  0.0 238.4 jit_solution(1437240349066409731)
XLA Ops:
  10.2 2.1 copy.37
  12.3 23.4 %all-gather.5.cloned.1.call-done = bf16[1536,768]{1,0:T(8,128)(2,1)} async-done(((bf16[384,768]{1,0:T(8,128)(2,1)}), bf16[1536,768]{1,0:T(8,128)(2,1)}) %all-gather.5.cloned.1.call-update) | async-done | bytes 2359312 | tf_op jit(solution)/shard_map/all_gather | solution.py:107
  35.7 2.1 fusion.16
  37.8 5.2 %all-gather = bf16[4,2,768]{2,1,0:T(2,128)(2,1)S(1)} all-gather(bf16[1,2,768]{2,1,0:T(2,128)(2,1)S(1)} %fusion.16), channel_id=1, replica_groups=mesh['group'=2,'seq'=4,'fsdp'=4] {'fsdp'}, dimensions={0}, use_global_device_ids=true | all-gather | bytes 15360 | tf_op jit(solution)/shard_map/all_gather | solution.py:114
  45.0 3.3 %all-to-all-start = ((bf16[8,12,384]{2,1,0:T(8,128)(2,1)}), bf16[8,12,384]{2,1,0:T(8,128)(2,1)S(1)}, u32[]{:S(2)}, u32[]{:S(2)}) async-start(bf16[8,12,384]{2,1,0:T(8,128)(2,1)} %copy.39), calls=%async_computation | async-start | bytes 196608 | tf_op jit(solution)/shard_map/all_to_all | solution.py:121
  49.0 5.0 %all-to-all-done = bf16[8,12,384]{2,1,0:T(8,128)(2,1)S(1)} async-done(((bf16[8,12,384]{2,1,0:T(8,128)(2,1)}), bf16[8,12,384]{2,1,0:T(8,128)(2,1)S(1)}, u32[]{:S(2)}, u32[]{:S(2)}) %all-to-all-start) | async-done | bytes 73760 | tf_op jit(solution)/shard_map/all_to_all | solution.py:121
  55.7 2.1 reshape.360
  57.8 3.3 %all-to-all-start.1 = ((bf16[4,2,4608]{2,1,0:T(2,128)(2,1)}), bf16[4,2,4608]{2,1,0:T(2,128)(2,1)S(1)}, u32[]{:S(2)}, u32[]{:S(2)}) async-start(bf16[4,2,4608]{2,1,0:T(2,128)(2,1)} %reshape.360), calls=%async_computation.1 | async-start | bytes 147456 | tf_op jit(solution)/shard_map/all_to_all | solution.py:130
  62.7 2.5 %all-to-all-done.1 = bf16[4,2,4608]{2,1,0:T(2,128)(2,1)S(1)} async-done(((bf16[4,2,4608]{2,1,0:T(2,128)(2,1)}), bf16[4,2,4608]{2,1,0:T(2,128)(2,1)S(1)}, u32[]{:S(2)}, u32[]{:S(2)}) %all-to-all-start.1) | async-done | bytes 73760 | tf_op jit(solution)/shard_map/all_to_all | solution.py:130
  65.2 1.8 reshape.361
  68.2 10.9 %all-reduce.3 = bf16[8,768]{1,0:T(8,128)(2,1)S(1)} all-reduce(bf16[8,768]{1,0:T(8,128)(2,1)S(1)} %convert_element_type.110), channel_id=2, replica_groups=mesh['group'=2,'seq'=4,'fsdp'=4] {'fsdp'}, use_global_device_ids=true, to_apply=%region_3.0.clone | all-reduce | flops 6144 | bytes 24576
  79.2 9.0 %all-gather.9.cloned.1.call-done = bf16[1536,768]{1,0:T(8,128)(2,1)} async-done(((bf16[384,768]{1,0:T(8,128)(2,1)}), bf16[1536,768]{1,0:T(8,128)(2,1)}) %all-gather.9.cloned.1.call-update) | async-done | bytes 2359312 | tf_op jit(solution)/shard_map/all_gather | solution.py:109
  88.2 3.2 %fusion.15 = bf16[2,768]{1,0:T(2,128)(2,1)S(1)} fusion(bf16[1536,768]{1,0:T(8,128)(2,1)} %all-gather.9.cloned.1.call-done, bf16[768,1536]{1,0:T(8,128)(2,1)} %all-gather.7.cloned.1.call-done, f32[2,1,1536]{2,1,0:T(1,128)S(1)} %slice_convert_fusion, pred[2]{0:T(512)(128)(4,1)S(1)} %fusion.57, bf16[8,768]{1,0:T(8,128)(2,1)S(1)} %all-reduce.3, u32[]{:T(128)S(6)} %multiply.36), kind=kOutput, calls=%fused_computation.30 | convolution fusion | flops 9446400 | bytes 4737540 | tf_op jit(solution)/shard_map/dot_general | solution.py:148
  91.4 3.2 %collective-permute-start = (bf16[2,768]{1,0:T(2,128)(2,1)S(1)}, bf16[2,768]{1,0:T(2,128)(2,1)S(1)}, u32[]{:S(2)}, u32[]{:S(2)}) collective-permute-start(bf16[2,768]{1,0:T(2,128)(2,1)S(1)} %fusion.15), channel_id=1, source_target_pairs={{0,15},{1,0},{2,1},{3,2},{4,3},{5,4},{6,5},{7,6},{8,7},{9,8},{10,9... | collective-permute-start | bytes 9224 | tf_op jit(solution)/shard_map/ppermute | solution.py:18
  95.9 4.4 %collective-permute-start.1 = (bf16[2,768]{1,0:T(2,128)(2,1)S(1)}, bf16[2,768]{1,0:T(2,128)(2,1)S(1)}, u32[]{:S(2)}, u32[]{:S(2)}) collective-permute-start(bf16[2,768]{1,0:T(2,128)(2,1)S(1)} %collective-permute-done), channel_id=1, source_target_pairs={{0,15},{1,0},{2,1},{3,2},{4,3},{5,4},{6,5},{7,6},{8,7},{9,8},{10,9... | collective-permute-start | bytes 9224 | tf_op jit(solution)/shard_map/ppermute | solution.py:18
  101.6 4.4 %collective-permute-start.2 = (bf16[2,768]{1,0:T(2,128)(2,1)S(1)}, bf16[2,768]{1,0:T(2,128)(2,1)S(1)}, u32[]{:S(2)}, u32[]{:S(2)}) collective-permute-start(bf16[2,768]{1,0:T(2,128)(2,1)S(1)} %collective-permute-done.1), channel_id=1, source_target_pairs={{0,15},{1,0},{2,1},{3,2},{4,3},{5,4},{6,5},{7,6},{8,7},{9,8},{10,9... | collective-permute-start | bytes 9224 | tf_op jit(solution)/shard_map/ppermute | solution.py:18
  107.3 4.4 %collective-permute-start.3 = (bf16[2,768]{1,0:T(2,128)(2,1)S(1)}, bf16[2,768]{1,0:T(2,128)(2,1)S(1)}, u32[]{:S(2)}, u32[]{:S(2)}) collective-permute-start(bf16[2,768]{1,0:T(2,128)(2,1)S(1)} %collective-permute-done.2), channel_id=1, source_target_pairs={{0,15},{1,0},{2,1},{3,2},{4,3},{5,4},{6,5},{7,6},{8,7},{9,8},{10,9... | collective-permute-start | bytes 9224 | tf_op jit(solution)/shard_map/ppermute | solution.py:18
  113.1 4.4 %collective-permute-start.4 = (bf16[2,768]{1,0:T(2,128)(2,1)S(1)}, bf16[2,768]{1,0:T(2,128)(2,1)S(1)}, u32[]{:S(2)}, u32[]{:S(2)}) collective-permute-start(bf16[2,768]{1,0:T(2,128)(2,1)S(1)} %collective-permute-done.3), channel_id=1, source_target_pairs={{0,15},{1,0},{2,1},{3,2},{4,3},{5,4},{6,5},{7,6},{8,7},{9,8},{10,9... | collective-permute-start | bytes 9224 | tf_op jit(solution)/shard_map/ppermute | solution.py:18
  117.8 7.6 %all-reduce.4 = (s32[32]{0:T(128)S(1)}, s32[32]{0:T(128)S(1)}) all-reduce(s32[32]{0:T(128)S(1)} %dynamic-update-slice, s32[32]{0:T(128)S(1)} %fusion.56), channel_id=1, replica_groups=mesh['group'=2,'seq'=4,'fsdp'=4] {'seq','fsdp'}, use_global_device_ids=true, to_apply=%add | all-reduce | flops 64 | bytes 512
  125.4 1.9 collective-permute-start.5
  129.0 6.8 %all-reduce.2 = s32[32]{0:T(128)S(1)} all-reduce(s32[32]{0:T(128)S(1)} %dynamic-update-slice.2), channel_id=1, replica_groups=mesh['group'=2,'seq'=4,'fsdp'=4] {'seq'}, use_global_device_ids=true, to_apply=%add.2 | all-reduce | flops 32 | bytes 256
  137.4 4.4 %collective-permute-start.7 = (bf16[2,768]{1,0:T(2,128)(2,1)S(1)}, bf16[2,768]{1,0:T(2,128)(2,1)S(1)}, u32[]{:S(2)}, u32[]{:S(2)}) collective-permute-start(bf16[2,768]{1,0:T(2,128)(2,1)S(1)} %collective-permute-done.6), channel_id=1, source_target_pairs={{0,15},{1,0},{2,1},{3,2},{4,3},{5,4},{6,5},{7,6},{8,7},{9,8},{10,9... | collective-permute-start | bytes 9224 | tf_op jit(solution)/shard_map/ppermute | solution.py:18
  143.2 4.4 %collective-permute-start.8 = (bf16[2,768]{1,0:T(2,128)(2,1)S(1)}, bf16[2,768]{1,0:T(2,128)(2,1)S(1)}, u32[]{:S(2)}, u32[]{:S(2)}) collective-permute-start(bf16[2,768]{1,0:T(2,128)(2,1)S(1)} %collective-permute-done.7), channel_id=1, source_target_pairs={{0,15},{1,0},{2,1},{3,2},{4,3},{5,4},{6,5},{7,6},{8,7},{9,8},{10,9... | collective-permute-start | bytes 9224 | tf_op jit(solution)/shard_map/ppermute | solution.py:18
  148.9 4.4 %collective-permute-start.9 = (bf16[2,768]{1,0:T(2,128)(2,1)S(1)}, bf16[2,768]{1,0:T(2,128)(2,1)S(1)}, u32[]{:S(2)}, u32[]{:S(2)}) collective-permute-start(bf16[2,768]{1,0:T(2,128)(2,1)S(1)} %collective-permute-done.8), channel_id=1, source_target_pairs={{0,15},{1,0},{2,1},{3,2},{4,3},{5,4},{6,5},{7,6},{8,7},{9,8},{10,9... | collective-permute-start | bytes 9224 | tf_op jit(solution)/shard_map/ppermute | solution.py:18
  154.6 4.4 %collective-permute-start.10 = (bf16[2,768]{1,0:T(2,128)(2,1)S(1)}, bf16[2,768]{1,0:T(2,128)(2,1)S(1)}, u32[]{:S(2)}, u32[]{:S(2)}) collective-permute-start(bf16[2,768]{1,0:T(2,128)(2,1)S(1)} %collective-permute-done.9), channel_id=1, source_target_pairs={{0,15},{1,0},{2,1},{3,2},{4,3},{5,4},{6,5},{7,6},{8,7},{9,8},{10,9... | collective-permute-start | bytes 9224 | tf_op jit(solution)/shard_map/ppermute | solution.py:18
  160.3 4.4 %collective-permute-start.11 = (bf16[2,768]{1,0:T(2,128)(2,1)S(1)}, bf16[2,768]{1,0:T(2,128)(2,1)S(1)}, u32[]{:S(2)}, u32[]{:S(2)}) collective-permute-start(bf16[2,768]{1,0:T(2,128)(2,1)S(1)} %collective-permute-done.10), channel_id=1, source_target_pairs={{0,15},{1,0},{2,1},{3,2},{4,3},{5,4},{6,5},{7,6},{8,7},{9,8},{10,9... | collective-permute-start | bytes 9224 | tf_op jit(solution)/shard_map/ppermute | solution.py:18
  166.0 4.4 %collective-permute-start.12 = (bf16[2,768]{1,0:T(2,128)(2,1)S(1)}, bf16[2,768]{1,0:T(2,128)(2,1)S(1)}, u32[]{:S(2)}, u32[]{:S(2)}) collective-permute-start(bf16[2,768]{1,0:T(2,128)(2,1)S(1)} %collective-permute-done.11), channel_id=1, source_target_pairs={{0,15},{1,0},{2,1},{3,2},{4,3},{5,4},{6,5},{7,6},{8,7},{9,8},{10,9... | collective-permute-start | bytes 9224 | tf_op jit(solution)/shard_map/ppermute | solution.py:18
  171.8 4.4 %collective-permute-start.13 = (bf16[2,768]{1,0:T(2,128)(2,1)S(1)}, bf16[2,768]{1,0:T(2,128)(2,1)S(1)}, u32[]{:S(2)}, u32[]{:S(2)}) collective-permute-start(bf16[2,768]{1,0:T(2,128)(2,1)S(1)} %collective-permute-done.12), channel_id=1, source_target_pairs={{0,15},{1,0},{2,1},{3,2},{4,3},{5,4},{6,5},{7,6},{8,7},{9,8},{10,9... | collective-permute-start | bytes 9224 | tf_op jit(solution)/shard_map/ppermute | solution.py:18
  177.5 4.4 %collective-permute-start.14 = (bf16[2,768]{1,0:T(2,128)(2,1)S(1)}, bf16[2,768]{1,0:T(2,128)(2,1)S(1)}, u32[]{:S(2)}, u32[]{:S(2)}) collective-permute-start(bf16[2,768]{1,0:T(2,128)(2,1)S(1)} %collective-permute-done.13), channel_id=1, source_target_pairs={{0,15},{1,0},{2,1},{3,2},{4,3},{5,4},{6,5},{7,6},{8,7},{9,8},{10,9... | collective-permute-start | bytes 9224 | tf_op jit(solution)/shard_map/ppermute | solution.py:18
  184.5 13.3 %all_gather.35 = bf16[32,192]{1,0:T(8,128)(2,1)S(1)} all-gather(bf16[8,192]{1,0:T(8,128)(2,1)S(1)} %convolution_convert_fusion.5), channel_id=1, replica_groups=mesh['group'=2,'seq'=4,'fsdp'=4] {'seq'}, dimensions={0}, use_global_device_ids=true | all-gather | bytes 15360 | tf_op jit(solution)/shard_map/all_gather | solution.py:182
  198.1 13.3 %all_gather.32 = bf16[32,192]{1,0:T(8,128)(2,1)S(1)} all-gather(bf16[8,192]{1,0:T(8,128)(2,1)S(1)} %convolution_convert_fusion.7), channel_id=1, replica_groups=mesh['group'=2,'seq'=4,'fsdp'=4] {'seq'}, dimensions={0}, use_global_device_ids=true | all-gather | bytes 15360 | tf_op jit(solution)/shard_map/all_gather | solution.py:183
  213.1 17.2 %reduce-scatter.4.cloned.1.call-done = bf16[192,8]{1,0:T(8,128)(2,1)} async-done(((bf16[768,8]{1,0:T(8,128)(2,1)}), bf16[192,8]{1,0:T(8,128)(2,1)}) %reduce-scatter.4.cloned.1.call-update) | async-done | bytes 3088
  (113 shorter events, 32.4 us)
Async XLA Ops:
  6.5 205.6 %copy-start = (bf16[192,768]{1,0:T(8,128)(2,1)S(1)}, bf16[192,768]{1,0:T(8,128)(2,1)}, u32[]{:S(2)}) copy-start(bf16[192,768]{1,0:T(8,128)(2,1)} %param.25) | copy-start | bytes 884740
  6.5 3.1 %copy-start.3 = (f32[1536]{0:T(1024)S(1)}, f32[1536]{0:T(1024)}, u32[]{:S(2)}) copy-start(f32[1536]{0:T(1024)} %param.15) | copy-start | bytes 18436
  6.5 29.2 %all-gather.5.cloned.1.call-start = ((), (), s32[]{:S(2)}) async-start(), calls=%async_computation.3 | async-start | bytes 2949120 | tf_op jit(solution)/shard_map/all_gather | solution.py:107
  7.3 71.9 %all-gather.7.cloned.1.call-start = ((), (), s32[]{:S(2)}) async-start(), calls=%async_computation.4 | async-start | bytes 2949120 | tf_op jit(solution)/shard_map/all_gather | solution.py:108
  8.0 80.2 %all-gather.9.cloned.1.call-start = ((), (), s32[]{:S(2)}) async-start(), calls=%async_computation.5 | async-start | bytes 2949120 | tf_op jit(solution)/shard_map/all_gather | solution.py:109
  45.0 9.0 %all-to-all-start = ((bf16[8,12,384]{2,1,0:T(8,128)(2,1)}), bf16[8,12,384]{2,1,0:T(8,128)(2,1)S(1)}, u32[]{:S(2)}, u32[]{:S(2)}) async-start(bf16[8,12,384]{2,1,0:T(8,128)(2,1)} %copy.39), calls=%async_computation | async-start | bytes 196608 | tf_op jit(solution)/shard_map/all_to_all | solution.py:121
  54.1 7.1 %copy-start.2 = (bf16[384,768]{1,0:T(8,128)(2,1)S(1)}, bf16[384,768]{1,0:T(8,128)(2,1)}, u32[]{:S(2)}) copy-start(bf16[384,768]{1,0:T(8,128)(2,1)} %param.18) | copy-start | bytes 1769476
  54.6 6.8 %copy-start.11 = (u32[32]{0:T(128)S(1)}, u32[32]{0:T(128)}, u32[]{:S(2)}) copy-start(u32[32]{0:T(128)} %constant.139) | copy-start | bytes 388
  57.8 7.4 %all-to-all-start.1 = ((bf16[4,2,4608]{2,1,0:T(2,128)(2,1)}), bf16[4,2,4608]{2,1,0:T(2,128)(2,1)S(1)}, u32[]{:S(2)}, u32[]{:S(2)}) async-start(bf16[4,2,4608]{2,1,0:T(2,128)(2,1)} %reshape.360), calls=%async_computation.1 | async-start | bytes 147456 | tf_op jit(solution)/shard_map/all_to_all | solution.py:130
  61.1 169.2 %reduce-scatter.4.cloned.1.call-start = ((), (), s32[]{:S(2)}) async-start(), calls=%async_computation.6 | async-start | bytes 245760
  79.1 32.6 %copy-start.10 = (u32[32]{0:T(128)S(1)}, u32[32]{0:T(128)}, u32[]{:S(2)}) copy-start(u32[32]{0:T(128)} %constant.121) | copy-start | bytes 388
  79.1 38.4 %copy-start.8 = (s32[2]{0:T(128)S(1)}, s32[2]{0:T(128)}, u32[]{:S(2)}) copy-start(s32[2]{0:T(128)} %param.26) | copy-start | bytes 28
  79.1 48.4 %copy-start.9 = (u32[32]{0:T(128)S(1)}, u32[32]{0:T(128)}, u32[]{:S(2)}) copy-start(u32[32]{0:T(128)} %constant.131) | copy-start | bytes 388
  79.1 104.9 %copy-start.4 = (bf16[768,192]{0,1:T(8,128)(2,1)S(1)}, bf16[768,192]{0,1:T(8,128)(2,1)}, u32[]{:S(2)}) copy-start(bf16[768,192]{0,1:T(8,128)(2,1)} %param.22) | copy-start | bytes 884740
  79.1 104.9 %copy-start.7 = (f32[768]{0:T(1024)S(1)}, f32[768]{0:T(1024)}, u32[]{:S(2)}) copy-start(f32[768]{0:T(1024)} %param.21) | copy-start | bytes 9220
  79.1 105.1 %copy-start.5 = (bf16[768,192]{0,1:T(8,128)(2,1)S(1)}, bf16[768,192]{0,1:T(8,128)(2,1)}, u32[]{:S(2)}) copy-start(bf16[768,192]{0,1:T(8,128)(2,1)} %param.23) | copy-start | bytes 884740
  79.2 118.8 %copy-start.6 = (bf16[768,192]{0,1:T(8,128)(2,1)S(1)}, bf16[768,192]{0,1:T(8,128)(2,1)}, u32[]{:S(2)}) copy-start(bf16[768,192]{0,1:T(8,128)(2,1)} %param.24) | copy-start | bytes 884740
  91.4 4.5 %collective-permute-start = (bf16[2,768]{1,0:T(2,128)(2,1)S(1)}, bf16[2,768]{1,0:T(2,128)(2,1)S(1)}, u32[]{:S(2)}, u32[]{:S(2)}) collective-permute-start(bf16[2,768]{1,0:T(2,128)(2,1)S(1)} %fusion.15), channel_id=1, source_target_pairs={{0,15},{1,0},{2,1},{3,2},{4,3},{5,4},{6,5},{7,6},{8,7},{9,8},{10,9... | collective-permute-start | bytes 9224 | tf_op jit(solution)/shard_map/ppermute | solution.py:18
  95.9 5.7 %collective-permute-start.1 = (bf16[2,768]{1,0:T(2,128)(2,1)S(1)}, bf16[2,768]{1,0:T(2,128)(2,1)S(1)}, u32[]{:S(2)}, u32[]{:S(2)}) collective-permute-start(bf16[2,768]{1,0:T(2,128)(2,1)S(1)} %collective-permute-done), channel_id=1, source_target_pairs={{0,15},{1,0},{2,1},{3,2},{4,3},{5,4},{6,5},{7,6},{8,7},{9,8},{10,9... | collective-permute-start | bytes 9224 | tf_op jit(solution)/shard_map/ppermute | solution.py:18
  101.6 5.7 %collective-permute-start.2 = (bf16[2,768]{1,0:T(2,128)(2,1)S(1)}, bf16[2,768]{1,0:T(2,128)(2,1)S(1)}, u32[]{:S(2)}, u32[]{:S(2)}) collective-permute-start(bf16[2,768]{1,0:T(2,128)(2,1)S(1)} %collective-permute-done.1), channel_id=1, source_target_pairs={{0,15},{1,0},{2,1},{3,2},{4,3},{5,4},{6,5},{7,6},{8,7},{9,8},{10,9... | collective-permute-start | bytes 9224 | tf_op jit(solution)/shard_map/ppermute | solution.py:18
  107.3 5.7 %collective-permute-start.3 = (bf16[2,768]{1,0:T(2,128)(2,1)S(1)}, bf16[2,768]{1,0:T(2,128)(2,1)S(1)}, u32[]{:S(2)}, u32[]{:S(2)}) collective-permute-start(bf16[2,768]{1,0:T(2,128)(2,1)S(1)} %collective-permute-done.2), channel_id=1, source_target_pairs={{0,15},{1,0},{2,1},{3,2},{4,3},{5,4},{6,5},{7,6},{8,7},{9,8},{10,9... | collective-permute-start | bytes 9224 | tf_op jit(solution)/shard_map/ppermute | solution.py:18
  113.1 12.4 %collective-permute-start.4 = (bf16[2,768]{1,0:T(2,128)(2,1)S(1)}, bf16[2,768]{1,0:T(2,128)(2,1)S(1)}, u32[]{:S(2)}, u32[]{:S(2)}) collective-permute-start(bf16[2,768]{1,0:T(2,128)(2,1)S(1)} %collective-permute-done.3), channel_id=1, source_target_pairs={{0,15},{1,0},{2,1},{3,2},{4,3},{5,4},{6,5},{7,6},{8,7},{9,8},{10,9... | collective-permute-start | bytes 9224 | tf_op jit(solution)/shard_map/ppermute | solution.py:18
  125.4 10.3 %collective-permute-start.5 = (bf16[2,768]{1,0:T(2,128)(2,1)S(1)}, bf16[2,768]{1,0:T(2,128)(2,1)S(1)}, u32[]{:S(2)}, u32[]{:S(2)}) collective-permute-start(bf16[2,768]{1,0:T(2,128)(2,1)S(1)} %collective-permute-done.4), channel_id=1, source_target_pairs={{0,15},{1,0},{2,1},{3,2},{4,3},{5,4},{6,5},{7,6},{8,7},{9,8},{10,9... | collective-permute-start | bytes 9224 | tf_op jit(solution)/shard_map/ppermute | solution.py:18
  135.8 1.7 collective-permute-start.6
  137.4 5.7 %collective-permute-start.7 = (bf16[2,768]{1,0:T(2,128)(2,1)S(1)}, bf16[2,768]{1,0:T(2,128)(2,1)S(1)}, u32[]{:S(2)}, u32[]{:S(2)}) collective-permute-start(bf16[2,768]{1,0:T(2,128)(2,1)S(1)} %collective-permute-done.6), channel_id=1, source_target_pairs={{0,15},{1,0},{2,1},{3,2},{4,3},{5,4},{6,5},{7,6},{8,7},{9,8},{10,9... | collective-permute-start | bytes 9224 | tf_op jit(solution)/shard_map/ppermute | solution.py:18
  143.2 5.7 %collective-permute-start.8 = (bf16[2,768]{1,0:T(2,128)(2,1)S(1)}, bf16[2,768]{1,0:T(2,128)(2,1)S(1)}, u32[]{:S(2)}, u32[]{:S(2)}) collective-permute-start(bf16[2,768]{1,0:T(2,128)(2,1)S(1)} %collective-permute-done.7), channel_id=1, source_target_pairs={{0,15},{1,0},{2,1},{3,2},{4,3},{5,4},{6,5},{7,6},{8,7},{9,8},{10,9... | collective-permute-start | bytes 9224 | tf_op jit(solution)/shard_map/ppermute | solution.py:18
  148.9 5.7 %collective-permute-start.9 = (bf16[2,768]{1,0:T(2,128)(2,1)S(1)}, bf16[2,768]{1,0:T(2,128)(2,1)S(1)}, u32[]{:S(2)}, u32[]{:S(2)}) collective-permute-start(bf16[2,768]{1,0:T(2,128)(2,1)S(1)} %collective-permute-done.8), channel_id=1, source_target_pairs={{0,15},{1,0},{2,1},{3,2},{4,3},{5,4},{6,5},{7,6},{8,7},{9,8},{10,9... | collective-permute-start | bytes 9224 | tf_op jit(solution)/shard_map/ppermute | solution.py:18
  154.6 5.7 %collective-permute-start.10 = (bf16[2,768]{1,0:T(2,128)(2,1)S(1)}, bf16[2,768]{1,0:T(2,128)(2,1)S(1)}, u32[]{:S(2)}, u32[]{:S(2)}) collective-permute-start(bf16[2,768]{1,0:T(2,128)(2,1)S(1)} %collective-permute-done.9), channel_id=1, source_target_pairs={{0,15},{1,0},{2,1},{3,2},{4,3},{5,4},{6,5},{7,6},{8,7},{9,8},{10,9... | collective-permute-start | bytes 9224 | tf_op jit(solution)/shard_map/ppermute | solution.py:18
  160.3 5.7 %collective-permute-start.11 = (bf16[2,768]{1,0:T(2,128)(2,1)S(1)}, bf16[2,768]{1,0:T(2,128)(2,1)S(1)}, u32[]{:S(2)}, u32[]{:S(2)}) collective-permute-start(bf16[2,768]{1,0:T(2,128)(2,1)S(1)} %collective-permute-done.10), channel_id=1, source_target_pairs={{0,15},{1,0},{2,1},{3,2},{4,3},{5,4},{6,5},{7,6},{8,7},{9,8},{10,9... | collective-permute-start | bytes 9224 | tf_op jit(solution)/shard_map/ppermute | solution.py:18
  166.0 5.7 %collective-permute-start.12 = (bf16[2,768]{1,0:T(2,128)(2,1)S(1)}, bf16[2,768]{1,0:T(2,128)(2,1)S(1)}, u32[]{:S(2)}, u32[]{:S(2)}) collective-permute-start(bf16[2,768]{1,0:T(2,128)(2,1)S(1)} %collective-permute-done.11), channel_id=1, source_target_pairs={{0,15},{1,0},{2,1},{3,2},{4,3},{5,4},{6,5},{7,6},{8,7},{9,8},{10,9... | collective-permute-start | bytes 9224 | tf_op jit(solution)/shard_map/ppermute | solution.py:18
  171.8 5.7 %collective-permute-start.13 = (bf16[2,768]{1,0:T(2,128)(2,1)S(1)}, bf16[2,768]{1,0:T(2,128)(2,1)S(1)}, u32[]{:S(2)}, u32[]{:S(2)}) collective-permute-start(bf16[2,768]{1,0:T(2,128)(2,1)S(1)} %collective-permute-done.12), channel_id=1, source_target_pairs={{0,15},{1,0},{2,1},{3,2},{4,3},{5,4},{6,5},{7,6},{8,7},{9,8},{10,9... | collective-permute-start | bytes 9224 | tf_op jit(solution)/shard_map/ppermute | solution.py:18
  177.5 5.7 %collective-permute-start.14 = (bf16[2,768]{1,0:T(2,128)(2,1)S(1)}, bf16[2,768]{1,0:T(2,128)(2,1)S(1)}, u32[]{:S(2)}, u32[]{:S(2)}) collective-permute-start(bf16[2,768]{1,0:T(2,128)(2,1)S(1)} %collective-permute-done.13), channel_id=1, source_target_pairs={{0,15},{1,0},{2,1},{3,2},{4,3},{5,4},{6,5},{7,6},{8,7},{9,8},{10,9... | collective-permute-start | bytes 9224 | tf_op jit(solution)/shard_map/ppermute | solution.py:18
  (1 other events, 2.2 us)
Sparse Core Ops, SparseCore 0:
  8.9 26.7 all-gather.4
  37.3 25.0 all-gather.6
  64.0 24.2 all-gather.8
  213.2 16.9 reduce-scatter.3
